TPU v7x, 32 devices: a whole 2x2x4 slice. The times are simulated.
32 devices in a mesh: groups: 2 (over y), ctx: 4 (over z), head: 2 (over x), sub: 2 (over core).
Axes of the slice: x: 2, y: 2, z: 4, core: 2. Of those that a mesh axis runs over, the one named last changes fastest.
Arguments:
- queries: bfloat16 [3072, 8192], P(('groups', 'ctx'), ('head', 'sub')), parts along dimension 0, may hold values from -60 to 60
- key_rows: bfloat16 [3072, 1024], P(('groups', 'ctx'), 'head'), parts along dimension 0, may hold values from -6 to 6
- value_rows: bfloat16 [3072, 1024], P(('groups', 'ctx'), 'head'), parts along dimension 0, may hold values from -6 to 6
- out_weight: bfloat16 [8192, 5120], P(('head', 'sub'), 'ctx'), may hold values from -0.375 to 0.375
Outputs:
- mixed: bfloat16 [3072, 5120], P(('groups', 'ctx'), ('head', 'sub')), parts along dimension 0
There are 2 independent parts, one for each index of `groups`. A program takes and returns all parts, laid end to end along the dimension named above; an argument that names none is the same for every part. Nothing has to cross between parts.
All inputs are finite; a program needn't handle non-finite values.
Results may differ from a plain program's by a relative error of at most 0.02.
Values may be sent and summed in bfloat16 or wider, within the bound.
A program may use at most 128 MiB of HBM per device.

v0:
```python
import jax
import jax.numpy as jnp
from jax import lax
from jax.sharding import PartitionSpec as P

QH = 64
KVH = 8
HD = 128


def from_behind(block, axis, distance):
    devices = range(lax.axis_size(axis))
    route = [((i - distance) % len(devices), i) for i in devices]
    return lax.ppermute(block, axis, route)


def on_device(queries, key_rows, value_rows, out_weight):
    token_count = queries.shape[0]
    heads_here = queries.shape[1] // HD
    pairs_here = key_rows.shape[1] // HD
    group_ratio = QH // KVH
    pairs_read = max(heads_here // group_ratio, 1)
    per_pair = heads_here // pairs_read
    head_offset = lax.axis_index("sub") * heads_here // group_ratio
    keys_read = lax.dynamic_slice_in_dim(
        key_rows.reshape(token_count, pairs_here, HD), head_offset, pairs_read, 1
    )
    values_read = lax.dynamic_slice_in_dim(
        value_rows.reshape(token_count, pairs_here, HD), head_offset, pairs_read, 1
    )
    stacked = jnp.stack([keys_read, values_read])
    grouped = queries.reshape(token_count, pairs_read, per_pair, HD)
    factor = 1.0 / HD**0.5

    def absorb(running, key_block, value_block):
        old_max, old_sum, old_out = running
        scores = (
            jnp.einsum("tngd,knd->tngk", grouped, key_block, preferred_element_type=jnp.float32)
            * factor
        )
        new_max = jnp.maximum(old_max, jnp.max(scores, axis=-1))
        shrink = jnp.exp(old_max - new_max)
        expo = jnp.exp(scores - new_max[..., None])
        new_sum = old_sum * shrink + jnp.sum(expo, axis=-1)
        added = jnp.einsum(
            "tngk,knd->tngd",
            expo.astype(jnp.bfloat16),
            value_block,
            preferred_element_type=jnp.float32,
        )
        return (new_max, new_sum, old_out * shrink[..., None] + added)

    empty = (
        jnp.full((token_count, pairs_read, per_pair), -1e30, jnp.float32),
        jnp.zeros((token_count, pairs_read, per_pair), jnp.float32),
        jnp.zeros((token_count, pairs_read, per_pair, HD), jnp.float32),
    )
    cycle_size = lax.axis_size("ctx")

    def forward(blocks):
        return from_behind(blocks, "ctx", 1)

    def both_turn(turn_index, loop_state):
        ahead, behind, running = loop_state
        ahead = forward(ahead)
        behind = from_behind(behind, "ctx", -1)
        running = absorb(running, ahead[0], ahead[1])
        return (ahead, behind, absorb(running, behind[0], behind[1]))

    ahead, _, final = lax.fori_loop(
        0,
        (cycle_size - 1) // 2,
        both_turn,
        (stacked, stacked, absorb(empty, keys_read, values_read)),
    )
    ahead = forward(ahead)
    final = absorb(final, ahead[0], ahead[1])
    attended = (
        (final[2] / final[1][..., None]).astype(jnp.bfloat16).reshape(token_count, heads_here * HD)
    )
    partial_value = jnp.dot(
        attended,
        lax.all_gather(out_weight, "ctx", axis=1, tiled=True),
        preferred_element_type=jnp.float32,
    )
    summed = lax.psum_scatter(
        partial_value.astype(jnp.bfloat16), ("head", "sub"), scatter_dimension=1, tiled=True
    )
    return summed


def solution(mesh):
    return jax.shard_map(
        on_device,
        mesh=mesh,
        in_specs=(
            P(("groups", "ctx"), ("head", "sub")),
            P(("groups", "ctx"), "head"),
            P(("groups", "ctx"), "head"),
            P(("head", "sub"), "ctx"),
        ),
        out_specs=P(("groups", "ctx"), ("head", "sub")),
        check_vma=False,
    )
```

profile of v0, /device:TPU:0, one launch (start us, length us, event | category | flops | bytes accessed | tf_op | source)
XLA Modules:
  0.0 442.7 jit_solution(13286977916574830429)
XLA Ops:
  6.5 0.0 all-gather.2.cloned.1.call-start
  6.5 0.7 all-gather.2.cloned.1.call-update
  7.3 0.0 reduce-scatter.2.cloned.1.call-start
  7.3 1.2 copy.17
  8.5 1.2 copy.20
  9.8 0.2 copy.50
  10.0 0.2 copy.22
  10.2 3.1 collective-permute-start
  13.3 2.1 collective-permute-start.1
  15.4 0.0 copy-done
  15.4 0.4 copy.51
  15.8 1.5 bitcast_reduce_fusion.3
  17.4 8.0 %collective-permute-done = bf16[2,384,2,128]{3,1,2,0:T(8,128)(2,1)S(1)} collective-permute-done((bf16[2,384,2,128]{3,1,2,0:T(8,128)(2,1)S(1)}, bf16[2,384,2,128]{3,1,2,0:T(8,128)(2,1)S(1)}, u32[]{:S(2)}, u32[]{:S(2)}) %collective-permute-start) | collective-permute-done | bytes 393248 | tf_op jit(solution)/shard_map/while/body/eval_jaxpr/ppermute | solution.py:14
  25.3 0.0 collective-permute-start.2
  25.4 1.5 bitcast_reduce_fusion.2
  26.8 12.9 %collective-permute-done.1 = bf16[2,384,2,128]{3,1,2,0:T(8,128)(2,1)S(1)} collective-permute-done((bf16[2,384,2,128]{3,1,2,0:T(8,128)(2,1)S(1)}, bf16[2,384,2,128]{3,1,2,0:T(8,128)(2,1)S(1)}, u32[]{:S(2)}, u32[]{:S(2)}) %collective-permute-start.1) | collective-permute-done | bytes 393248 | tf_op jit(solution)/shard_map/while/body/eval_jaxpr/ppermute | solution.py:14
  39.7 5.1 %bitcast_reduce_fusion.1 = (f32[384,2,8]{0,2,1:T(8,128)S(1)}, f32[2,384,384,8]{2,1,3,0:T(8,128)}) fusion(bf16[384,2,8,128]{3,2,1,0:T(8,128)(2,1)S(1)} %bitcast.138, bf16[2,384,2,128]{3,1,2,0:T(8,128)(2,1)S(1)} %collective-permute-done.1), kind=kOutput, calls=%fused_computation.4 | convolution fusion | flops 608692224 | bytes 11231232 | tf_op jit(solution)/shard_map/while/body/eval_jaxpr/tngd,knd->tngk/dot_general | solution.py:38
  44.8 0.0 copy-done.1
  44.8 7.7 %collective-permute-done.2 = bf16[2,384,2,128]{3,1,2,0:T(8,128)(2,1)S(1)} collective-permute-done((bf16[2,384,2,128]{3,1,2,0:T(8,128)(2,1)S(1)}, bf16[2,384,2,128]{3,1,2,0:T(8,128)(2,1)S(1)}, u32[]{:S(2)}, u32[]{:S(2)}) %collective-permute-start.2) | collective-permute-done | bytes 393248 | tf_op jit(solution)/shard_map/ppermute | solution.py:14
  52.5 5.1 %bitcast_reduce_fusion = (f32[384,2,8]{0,2,1:T(8,128)S(1)}, f32[2,384,384,8]{2,1,3,0:T(8,128)}) fusion(bf16[384,2,8,128]{3,2,1,0:T(8,128)(2,1)S(1)} %bitcast.139, bf16[2,384,2,128]{3,1,2,0:T(8,128)(2,1)S(1)} %collective-permute-done.2), kind=kOutput, calls=%fused_computation.1 | convolution fusion | flops 608692224 | bytes 11231232 | tf_op jit(solution)/shard_map/tngd,knd->tngk/dot_general | solution.py:38
  57.6 0.0 copy-done.3
  57.6 1.6 fusion.4
  59.2 0.0 copy-done.5
  59.2 1.6 fusion.6
  60.8 5.3 %fusion.8 = f32[384,2,8]{0,2,1:T(8,128)S(1)} fusion(f32[2,384,384,8]{2,1,3,0:T(8,128)} %get-tuple-element.38, f32[384,2,8]{0,2,1:T(8,128)S(1)} %get-tuple-element.30), kind=kLoop, calls=%fused_computation.16 | loop fusion | flops 7071744 | bytes 9486336 | tf_op jit(solution)/shard_map/while/body/eval_jaxpr/reduce_sum | solution.py:44
  66.1 5.2 %fusion.10 = f32[384,2,8]{0,2,1:T(8,128)S(1)} fusion(f32[2,384,384,8]{2,1,3,0:T(8,128)} %get-tuple-element.36, f32[384,2,8]{0,2,1:T(8,128)S(1)} %get-tuple-element.28), kind=kLoop, calls=%fused_computation.18 | loop fusion | flops 7071744 | bytes 9486336 | tf_op jit(solution)/shard_map/reduce_sum | solution.py:44
  71.4 0.0 copy-start.2
  71.4 0.7 multiply_add_fusion
  72.0 2.0 fusion.18
  74.1 0.0 copy-done.2
  74.1 0.0 slice-start.2
  74.1 0.0 copy-start.4
  74.1 0.0 slice-start.3
  74.1 0.0 slice-start.4
  74.2 1.8 fusion.16
  75.9 0.1 slice-done.2
  76.0 0.1 copy-done.4
  76.1 0.0 copy-start.9
  76.1 0.0 copy-start.10
  76.1 1.7 fusion.14
  77.9 1.1 slice-done.5
  78.9 0.0 copy-done.6
  79.0 0.0 copy-done.10
  79.0 3.6 fusion.29
  82.6 296.6 %all-gather.2.cloned.1.call-done = bf16[2048,5120]{1,0:T(8,128)(2,1)} async-done(((bf16[2048,1280]{1,0:T(8,128)(2,1)}), bf16[2048,5120]{1,0:T(8,128)(2,1)}) %all-gather.2.cloned.1.call-update) | async-done | bytes 20971536 | tf_op jit(solution)/shard_map/all_gather | solution.py:83
  379.1 14.5 %convolution_convert_fusion = bf16[384,5120]{1,0:T(8,128)(2,1)} fusion(bf16[384,2048]{0,1:T(8,128)(2,1)} %bitcast.147, bf16[2048,5120]{1,0:T(8,128)(2,1)} %all-gather.2.cloned.1.call-done), kind=kOutput, calls=%fused_computation.20 | convolution fusion | flops 8055029760 | bytes 26476544 | tf_op jit(solution)/shard_map/dot_general | solution.py:81
  393.7 0.0 reduce-scatter.2.cloned.1.call-update
  393.7 42.2 %reduce-scatter.2.cloned.1.call-done = bf16[384,1280]{1,0:T(8,128)(2,1)} async-done(((bf16[384,5120]{1,0:T(8,128)(2,1)}), bf16[384,1280]{1,0:T(8,128)(2,1)}) %reduce-scatter.2.cloned.1.call-update) | async-done | bytes 983056 | tf_op jit(solution)/shard_map/reduce_scatter | solution.py:86
  (22 shorter events, 0.1 us)
Async XLA Ops:
  6.5 8.9 %copy-start = (bf16[384,2048]{1,0:T(8,128)(2,1)S(1)}, bf16[384,2048]{1,0:T(8,128)(2,1)}, u32[]{:S(2)}) copy-start(bf16[384,2048]{1,0:T(8,128)(2,1)} %param.4) | copy-start | bytes 4718596
  6.5 372.6 %all-gather.2.cloned.1.call-start = ((), (), s32[]{:S(2)}) async-start(), calls=%async_computation.1 | async-start | bytes 26214400 | tf_op jit(solution)/shard_map/all_gather | solution.py:83
  7.3 428.7 %reduce-scatter.2.cloned.1.call-start = ((), (), s32[]{:S(2)}) async-start(), calls=%async_computation.2 | async-start | bytes 4915200 | tf_op jit(solution)/shard_map/reduce_scatter | solution.py:86
  10.2 15.1 %collective-permute-start = (bf16[2,384,2,128]{3,1,2,0:T(8,128)(2,1)S(1)}, bf16[2,384,2,128]{3,1,2,0:T(8,128)(2,1)S(1)}, u32[]{:S(2)}, u32[]{:S(2)}) collective-permute-start(bf16[2,384,2,128]{3,1,2,0:T(8,128)(2,1)S(1)} %pad_maximum_fusion), channel_id=1, source_target_pairs={{12,0},{0,4},{4,8},{8,12},{13,1},{1,5},{5,9},{9,13},{14,2},{2,6},{... | collective-permute-start | bytes 1179656 | tf_op jit(solution)/shard_map/while/body/eval_jaxpr/ppermute | solution.py:14
  13.3 26.4 %collective-permute-start.1 = (bf16[2,384,2,128]{3,1,2,0:T(8,128)(2,1)S(1)}, bf16[2,384,2,128]{3,1,2,0:T(8,128)(2,1)S(1)}, u32[]{:S(2)}, u32[]{:S(2)}) collective-permute-start(bf16[2,384,2,128]{3,1,2,0:T(8,128)(2,1)S(1)} %pad_maximum_fusion), channel_id=1, source_target_pairs={{4,0},{8,4},{12,8},{0,12},{5,1},{9,5},{13,9},{1,13},{6,2},{10,6},{... | collective-permute-start | bytes 1179656 | tf_op jit(solution)/shard_map/while/body/eval_jaxpr/ppermute | solution.py:14
  25.3 19.5 %copy-start.1 = (bf16[2,384,2,128]{3,1,2,0:T(8,128)(2,1)}, bf16[2,384,2,128]{3,1,2,0:T(8,128)(2,1)S(1)}, u32[]{:S(2)}) copy-start(bf16[2,384,2,128]{3,1,2,0:T(8,128)(2,1)S(1)} %collective-permute-done) | copy-start | bytes 1179652
  25.3 27.2 %collective-permute-start.2 = (bf16[2,384,2,128]{3,1,2,0:T(8,128)(2,1)S(1)}, bf16[2,384,2,128]{3,1,2,0:T(8,128)(2,1)S(1)}, u32[]{:S(2)}, u32[]{:S(2)}) collective-permute-start(bf16[2,384,2,128]{3,1,2,0:T(8,128)(2,1)S(1)} %collective-permute-done), channel_id=1, source_target_pairs={{12,0},{0,4},{4,8},{8,12},{13,1},{1,5},{5,9},{9,13},{14,2},{2,6},{... | collective-permute-start | bytes 1179656 | tf_op jit(solution)/shard_map/ppermute | solution.py:14
  39.7 17.9 %copy-start.3 = (bf16[2,384,2,128]{3,1,2,0:T(8,128)(2,1)}, bf16[2,384,2,128]{3,1,2,0:T(8,128)(2,1)S(1)}, u32[]{:S(2)}) copy-start(bf16[2,384,2,128]{3,1,2,0:T(8,128)(2,1)S(1)} %collective-permute-done.1) | copy-start | bytes 1179652
  52.5 6.7 %copy-start.5 = (bf16[2,384,2,128]{3,1,2,0:T(8,128)(2,1)}, bf16[2,384,2,128]{3,1,2,0:T(8,128)(2,1)S(1)}, u32[]{:S(2)}) copy-start(bf16[2,384,2,128]{3,1,2,0:T(8,128)(2,1)S(1)} %collective-permute-done.2) | copy-start | bytes 1179652
  71.4 2.7 copy-start.2
  72.0 3.9 slice-start
  72.0 3.9 slice-start.1
  74.1 1.9 slice-start.2
  74.1 2.0 copy-start.4
  74.1 3.7 slice-start.3
  74.1 3.7 slice-start.4
  76.1 2.9 slice-start.5
  76.1 2.9 copy-start.6
  76.1 2.9 copy-start.7
  76.1 2.9 copy-start.8
  76.1 2.9 copy-start.9
  76.1 2.9 copy-start.10
Sparse Core Ops, SparseCore 0:
  8.9 370.1 all-gather.1
  393.8 42.0 reduce-scatter.1
where the time goes:
time: 443 us
  waiting for transfers between devices  368 us (83%)
  matrix products  36.8 us (8%)
  other arithmetic  14.5 us (3%)
  between operations  13.7 us (3%)
  starting transfers between devices  5.24 us (1%)
  local copies, waits for them, and re-layouts  4.47 us (1%)
    all_gather x1, waiting for transfers between devices, on_device(): lax.all_gather(out_weight, 'ctx', axis=1, tiled=True)  297 us
    reduce_scatter x1, waiting for transfers between devices, on_device(): lax.psum_scatter(partial_value.astype(jnp.bfloat16), ('head', 'sub'), sca...  42.2 us
    ppermute x3, waiting for transfers between devices, from_behind(): return lax.ppermute(block, axis, route)  28.6 us
    dot_general x1, matrix products, on_device(): jnp.dot(attended, lax.all_gather(out_weight, 'ctx', axis=1, tiled=True),...  14.5 us
    reduce_sum x4, other arithmetic, absorb(): new_sum = old_sum * shrink + jnp.sum(expo, axis=-1)  13.7 us
    dot_general x4, matrix products, absorb(): jnp.einsum('tngd,knd->tngk', grouped, key_block, preferred_element_type=j...  13.2 us
    dot_general x4, matrix products, absorb(): jnp.einsum('tngk,knd->tngd', expo.astype(jnp.bfloat16), value_block, pref...  9.13 us
  transfers between devices with their start and end apart: 5, of which 5 were waited for; matrix products, arithmetic and copies ran while one was open for 9% of the time, Pallas kernels for 0%

commit v1 on v0

--- a/solution.py
+++ b/solution.py
@@ -6,6 +6,12 @@
 QH = 64
 KVH = 8
 HD = 128
+
+
+def tiled_gather(x, axis, dim):
+    size = lax.axis_size(axis)
+    repeats = [size if d == dim else 1 for d in range(x.ndim)]
+    return lax.all_to_all(jnp.tile(x, repeats), axis, split_axis=dim, concat_axis=dim, tiled=True)
 
 
 def from_behind(block, axis, distance):
@@ -79,9 +85,7 @@
         (final[2] / final[1][..., None]).astype(jnp.bfloat16).reshape(token_count, heads_here * HD)
     )
     partial_value = jnp.dot(
-        attended,
-        lax.all_gather(out_weight, "ctx", axis=1, tiled=True),
-        preferred_element_type=jnp.float32,
+        attended, tiled_gather(out_weight, "ctx", 1), preferred_element_type=jnp.float32
     )
     summed = lax.psum_scatter(
         partial_value.astype(jnp.bfloat16), ("head", "sub"), scatter_dimension=1, tiled=True

time: 443 us -> 633 us (1.43)
  starting transfers between devices: 5.24 us -> 123 us
  waiting for transfers between devices: 368 us -> 402 us
  local copies, waits for them, and re-layouts: 4.47 us -> 37.5 us
    ppermute x3, waiting for transfers between devices: 28.6 us -> 353 us  [from_behind(): return lax.ppermute(block, axis, route)]
    all_gather x1 -> x0, waiting for transfers between devices: 297 us -> none  [on_device(): lax.all_gather(out_weight, 'ctx', axis=1, tiled=True)]
    ppermute x3, starting transfers between devices: 5.2 us -> 115 us  [from_behind(): return lax.ppermute(block, axis, route)]
    all_to_all x0 -> x1, local copies, waits for them, and re-layouts: none -> 27.2 us  [tiled_gather(): lax.all_to_all(jnp.tile(x, repeats), axis, split_axis=dim, concat_axis=di...]
    another operation x0 -> x1, local copies, waits for them, and re-layouts: none -> 9.06 us  [tiled_gather(): jnp.tile(x, repeats)]
    all_to_all x0 -> x1, starting transfers between devices: none -> 7.85 us  [tiled_gather(): lax.all_to_all(jnp.tile(x, repeats), axis, split_axis=dim, concat_axis=di...]
    dot_general x4, matrix products: 9.13 us -> 15.5 us  [absorb(): jnp.einsum('tngk,knd->tngd', expo.astype(jnp.bfloat16), value_block, pref...]
  transfers between devices with their start and end apart: 5 -> 5, of which waited for: 5 -> 3; matrix products, arithmetic and copies ran while one was open for 9% -> 7% of each run, Pallas kernels for 0% -> 0%
where the time goes in v1:
time: 633 us; the launch traced here: 632 us
  waiting for transfers between devices  402 us (64%)
  starting transfers between devices  123 us (19%)
  matrix products  42.6 us (7%)
  local copies, waits for them, and re-layouts  37.5 us (6%)
  other arithmetic  13.8 us (2%)
  between operations  13.6 us (2%)
    ppermute x3, waiting for transfers between devices, from_behind(): return lax.ppermute(block, axis, route)  353 us
    ppermute x3, starting transfers between devices, from_behind(): return lax.ppermute(block, axis, route)  115 us
    reduce_scatter x1, waiting for transfers between devices, on_device(): lax.psum_scatter(partial_value.astype(jnp.bfloat16), ('head', 'sub'), sca...  48.3 us
    all_to_all x1, local copies, waits for them, and re-layouts, tiled_gather(): lax.all_to_all(jnp.tile(x, repeats), axis, split_axis=dim, concat_axis=di...  27.2 us
    dot_general x4, matrix products, absorb(): jnp.einsum('tngk,knd->tngd', expo.astype(jnp.bfloat16), value_block, pref...  15.5 us
    dot_general x1, matrix products, on_device(): jnp.dot(attended, tiled_gather(out_weight, 'ctx', 1), preferred_element_t...  13.9 us
    reduce_sum x4, other arithmetic, absorb(): new_sum = old_sum * shrink + jnp.sum(expo, axis=-1)  13.7 us
    dot_general x4, matrix products, absorb(): jnp.einsum('tngd,knd->tngk', grouped, key_block, preferred_element_type=j...  13.2 us
  transfers between devices with their start and end apart: 5, of which 3 were waited for; matrix products, arithmetic and copies ran while one was open for 7% of the time, Pallas kernels for 0%

profile of v1, /device:TPU:0, one launch (start us, length us, event | category | flops | bytes accessed | tf_op | source)
XLA Modules:
  0.0 631.7 jit_solution(13459318429761866275)
XLA Ops:
  6.5 9.1 %tile.2 = bf16[2048,4,1280]{2,0,1:T(8,128)(2,1)} broadcast(bf16[2048,1280]{1,0:T(8,128)(2,1)} %param.7), dimensions={0,2} | broadcast | bytes 26214400 | tf_op jit(solution)/shard_map/tile | solution.py:14
  15.6 0.0 copy-start.1
  15.6 0.0 copy-start.2
  15.6 0.0 copy-start
  15.6 7.9 %all-to-all-start = ((bf16[2048,4,1280]{2,0,1:T(8,128)(2,1)}), bf16[2048,4,1280]{2,0,1:T(8,128)(2,1)}, u32[]{:S(2)}, u32[]{:S(2)}) async-start(bf16[2048,4,1280]{2,0,1:T(8,128)(2,1)} %tile.2), calls=%async_computation | async-start | bytes 41943040 | tf_op jit(solution)/shard_map/all_to_all | solution.py:14
  23.5 0.0 reduce-scatter.2.cloned.1.call-start
  23.5 0.0 copy-done.1
  23.5 0.2 copy.47
  23.8 0.0 copy-done.2
  23.8 0.2 copy.50
  24.0 0.2 copy.52
  24.2 0.2 copy.81
  24.4 5.0 collective-permute-start.1
  29.5 0.0 collective-permute-start
  29.5 0.0 copy-done
  29.5 0.4 copy.82
  29.9 1.5 bitcast_reduce_fusion.3
  31.4 352.0 %collective-permute-done = bf16[2,384,2,128]{3,1,2,0:T(8,128)(2,1)S(1)} collective-permute-done((bf16[2,384,2,128]{3,1,2,0:T(8,128)(2,1)S(1)}, bf16[2,384,2,128]{3,1,2,0:T(8,128)(2,1)S(1)}, u32[]{:S(2)}, u32[]{:S(2)}) %collective-permute-start) | collective-permute-done | bytes 393248 | tf_op jit(solution)/shard_map/while/body/eval_jaxpr/ppermute | solution.py:20
  383.4 109.8 %collective-permute-start.2 = (bf16[2,384,2,128]{3,1,2,0:T(8,128)(2,1)S(1)}, bf16[2,384,2,128]{3,1,2,0:T(8,128)(2,1)S(1)}, u32[]{:S(2)}, u32[]{:S(2)}) collective-permute-start(bf16[2,384,2,128]{3,1,2,0:T(8,128)(2,1)S(1)} %collective-permute-done), channel_id=1, source_target_pairs={{12,0},{0,4},{4,8},{8,12},{13,1},{1,5},{5,9},{9,13},{14,2},{2,6},{... | collective-permute-start | bytes 1179656 | tf_op jit(solution)/shard_map/ppermute | solution.py:20
  493.2 1.5 bitcast_reduce_fusion.2
  494.7 0.0 collective-permute-done.1
  494.7 5.1 bitcast_reduce_fusion.1
  499.8 1.2 collective-permute-done.2
  501.0 5.1 bitcast_reduce_fusion
  506.1 1.6 fusion.4
  507.7 5.3 fusion.10
  513.0 5.3 fusion.8
  518.3 1.6 fusion.6
  519.9 2.1 fusion.18
  521.9 5.4 fusion.14
  527.4 1.7 fusion.16
  529.1 6.3 fusion.29
  535.5 0.0 all-to-all-done
  535.5 27.2 %copy.62 = bf16[2048,4,1280]{0,2,1:T(8,128)(2,1)} copy(bf16[2048,4,1280]{2,0,1:T(8,128)(2,1)} %all-to-all-done) | data formatting | bytes 41943040 | tf_op jit(solution)/shard_map/all_to_all | solution.py:14
  562.7 13.9 %convolution_convert_fusion = bf16[384,5120]{1,0:T(8,128)(2,1)} fusion(bf16[384,2048]{0,1:T(8,128)(2,1)S(1)} %bitcast.145, bf16[2048,5120]{0,1:T(8,128)(2,1)} %bitcast.139), kind=kOutput, calls=%fused_computation.20 | convolution fusion | flops 8055029760 | bytes 26476544 | tf_op jit(solution)/shard_map/dot_general | solution.py:87
  576.6 0.0 reduce-scatter.2.cloned.1.call-update
  576.6 48.3 %reduce-scatter.2.cloned.1.call-done = bf16[384,1280]{1,0:T(8,128)(2,1)} async-done(((bf16[384,5120]{1,0:T(8,128)(2,1)}), bf16[384,1280]{1,0:T(8,128)(2,1)}) %reduce-scatter.2.cloned.1.call-update) | async-done | bytes 983056 | tf_op jit(solution)/shard_map/reduce_scatter | solution.py:90
  (4 shorter events, 0.1 us)
Async XLA Ops:
  15.6 7.9 %copy-start.1 = (bf16[384,512]{1,0:T(8,128)(2,1)S(1)}, bf16[384,512]{1,0:T(8,128)(2,1)}, u32[]{:S(2)}) copy-start(bf16[384,512]{1,0:T(8,128)(2,1)} %param.5) | copy-start | bytes 1179652
  15.6 8.2 %copy-start.2 = (bf16[384,512]{1,0:T(8,128)(2,1)S(1)}, bf16[384,512]{1,0:T(8,128)(2,1)}, u32[]{:S(2)}) copy-start(bf16[384,512]{1,0:T(8,128)(2,1)} %param.6) | copy-start | bytes 1179652
  15.6 13.9 %copy-start = (bf16[384,2048]{1,0:T(8,128)(2,1)S(1)}, bf16[384,2048]{1,0:T(8,128)(2,1)}, u32[]{:S(2)}) copy-start(bf16[384,2048]{1,0:T(8,128)(2,1)} %param.4) | copy-start | bytes 4718596
  15.6 519.9 %all-to-all-start = ((bf16[2048,4,1280]{2,0,1:T(8,128)(2,1)}), bf16[2048,4,1280]{2,0,1:T(8,128)(2,1)}, u32[]{:S(2)}, u32[]{:S(2)}) async-start(bf16[2048,4,1280]{2,0,1:T(8,128)(2,1)} %tile.2), calls=%async_computation | async-start | bytes 41943040 | tf_op jit(solution)/shard_map/all_to_all | solution.py:14
  23.5 601.4 %reduce-scatter.2.cloned.1.call-start = ((), (), s32[]{:S(2)}) async-start(), calls=%async_computation.2 | async-start | bytes 4915200 | tf_op jit(solution)/shard_map/reduce_scatter | solution.py:90
  24.4 470.3 %collective-permute-start.1 = (bf16[2,384,2,128]{3,1,2,0:T(8,128)(2,1)S(1)}, bf16[2,384,2,128]{3,1,2,0:T(8,128)(2,1)S(1)}, u32[]{:S(2)}, u32[]{:S(2)}) collective-permute-start(bf16[2,384,2,128]{3,1,2,0:T(8,128)(2,1)S(1)} %pad_maximum_fusion), channel_id=1, source_target_pairs={{4,0},{8,4},{12,8},{0,12},{5,1},{9,5},{13,9},{1,13},{6,2},{10,6},{... | collective-permute-start | bytes 1179656 | tf_op jit(solution)/shard_map/while/body/eval_jaxpr/ppermute | solution.py:20
  29.5 353.9 %collective-permute-start = (bf16[2,384,2,128]{3,1,2,0:T(8,128)(2,1)S(1)}, bf16[2,384,2,128]{3,1,2,0:T(8,128)(2,1)S(1)}, u32[]{:S(2)}, u32[]{:S(2)}) collective-permute-start(bf16[2,384,2,128]{3,1,2,0:T(8,128)(2,1)S(1)} %pad_maximum_fusion), channel_id=1, source_target_pairs={{12,0},{0,4},{4,8},{8,12},{13,1},{1,5},{5,9},{9,13},{14,2},{2,6},{... | collective-permute-start | bytes 1179656 | tf_op jit(solution)/shard_map/while/body/eval_jaxpr/ppermute | solution.py:20
  383.4 117.6 %collective-permute-start.2 = (bf16[2,384,2,128]{3,1,2,0:T(8,128)(2,1)S(1)}, bf16[2,384,2,128]{3,1,2,0:T(8,128)(2,1)S(1)}, u32[]{:S(2)}, u32[]{:S(2)}) collective-permute-start(bf16[2,384,2,128]{3,1,2,0:T(8,128)(2,1)S(1)} %collective-permute-done), channel_id=1, source_target_pairs={{12,0},{0,4},{4,8},{8,12},{13,1},{1,5},{5,9},{9,13},{14,2},{2,6},{... | collective-permute-start | bytes 1179656 | tf_op jit(solution)/shard_map/ppermute | solution.py:20
Sparse Core Ops, SparseCore 0:
  576.7 48.1 reduce-scatter.1
